TPU v7x, 32 devices: a whole 2x2x4 slice. The times are simulated.
32 devices in a mesh: dp: 8 (over z, y), tensor: 4 (over x, core).
Axes of the slice: x: 2, y: 2, z: 4, core: 2. Of those that a mesh axis runs over, the one named last changes fastest.
Arguments:
- block_input: bfloat16 [8192, 1536], P(('dp', 'tensor')), may hold values from -6 to 6
- segment_ids: int32 [8, 1024], P('dp'), may hold values from 0 to 3, as said below
- gain_attn: float32 [1536], replicated, may hold values from 0.5 to 1.5
- w_query: bfloat16 [1536, 1536], P('dp', 'tensor'), may hold values from -0.15625 to 0.15625
- b_query: float32 [1536], P('tensor'), may hold values from -3 to 3
- w_keyval: bfloat16 [1536, 512], P('dp'), may hold values from -0.15625 to 0.15625
- b_keyval: float32 [512], replicated, may hold values from -3 to 3
- w_out: bfloat16 [1536, 1536], P('tensor', 'dp'), may hold values from -0.625 to 0.625
- gain_ffn: float32 [1536], replicated, may hold values from 0.5 to 1.5
- w_gate: bfloat16 [1536, 8960], P('dp', 'tensor'), may hold values from -0.15625 to 0.15625
- w_up: bfloat16 [1536, 8960], P('dp', 'tensor'), may hold values from -0.15625 to 0.15625
- w_down: bfloat16 [8960, 1536], P('tensor', 'dp'), may hold values from -0.0625 to 0.0625
- cotangent: bfloat16 [8192, 1536], P(('dp', 'tensor')), may hold values from -6 to 6
Outputs:
- block_output: bfloat16 [8192, 1536], P(('dp', 'tensor'))
- grad_input: bfloat16 [8192, 1536], P(('dp', 'tensor'))
- grad_gain_attn: float32 [1536], P(('dp', 'tensor'))
- grad_w_query: float32 [1536, 1536], P('dp', 'tensor')
- grad_b_query: float32 [1536], P(('dp', 'tensor'))
- grad_w_keyval: float32 [1536, 512], P(('dp', 'tensor'))
- grad_b_keyval: float32 [512], P(('dp', 'tensor'))
- grad_w_out: float32 [1536, 1536], P('tensor', 'dp')
- grad_gain_ffn: float32 [1536], P(('dp', 'tensor'))
- grad_w_gate: float32 [1536, 8960], P('dp', 'tensor')
- grad_w_up: float32 [1536, 8960], P('dp', 'tensor')
- grad_w_down: float32 [8960, 1536], P('tensor', 'dp')
Inputs may be any that keep to these rules, and one draw needn't show every extreme that they name: `segment_ids`: ids start at 0 and never fall along a sequence, each rising by one at a document's start; a sequence holds 2 to 4 documents, each of 204 tokens or more; some sequence holds 4.
All inputs are finite; a program needn't handle non-finite values.
Results may differ from a plain program's by a relative error of at most 0.018.
Values may be sent and summed in bfloat16 or wider, within the bound.
No kernel may reach another device: no remote copies, remote signals or barrier semaphores. Data moves between devices by JAX's collectives and lax.ppermute only.
A program may use at most 256 MiB of HBM per device.

v0:
```python
import math
import jax
import jax.numpy as jnp
from jax import lax
from jax.sharding import PartitionSpec as P

HQ = 12
KV = 2
HD = 128
epsilon = 1e-06
rope_base = 1000000.0
masked_score = -1e30


def matmul(left, right):
    return jnp.dot(left, right, preferred_element_type=jnp.float32)


def positions_of(segment_row):
    index_row = jnp.arange(segment_row.shape[0], dtype=jnp.int32)
    starts = jnp.concatenate(
        [jnp.ones((1,), jnp.int32), (segment_row[1:] != segment_row[:-1]).astype(jnp.int32)]
    )
    first_index = lax.cummax(jnp.where(starts > 0, index_row, 0), axis=0)
    return index_row - first_index


def allowed_of(segment_row):
    index_row = jnp.arange(segment_row.shape[0], dtype=jnp.int32)
    causal = index_row[:, None] >= index_row[None, :]
    return causal & (segment_row[:, None] == segment_row[None, :])


def rotary(positions):
    inverse = rope_base ** (-(jnp.arange(HD // 2, dtype=jnp.float32) * 2.0 / HD))
    angles = positions.astype(jnp.float32)[:, None] * inverse[None, :]
    angles = jnp.concatenate([angles, angles], axis=1)
    return (jnp.cos(angles), jnp.sin(angles))


def turn(values_in, cosine_table, sine_table):
    half_size = values_in.shape[-1] // 2
    rolled = jnp.concatenate([-values_in[..., half_size:], values_in[..., :half_size]], axis=-1)
    return values_in * cosine_table + rolled * sine_table


def norm_forward(values_in):
    row_scale = lax.rsqrt(jnp.mean(values_in * values_in, axis=-1, keepdims=True) + epsilon)
    return (values_in * row_scale, row_scale)


def norm_backward(grad_out, normed, row_scale, gain_vec):
    grad_normed = grad_out * gain_vec
    grad_in = row_scale * (
        grad_normed - normed * jnp.mean(grad_normed * normed, axis=-1, keepdims=True)
    )
    return (grad_in, jnp.sum(grad_out * normed, axis=0))


def gather_three(first, second, third):
    return (
        lax.all_gather(first, "dp", axis=0, tiled=True),
        lax.all_gather(second, "dp", axis=0, tiled=True),
        lax.all_gather(third, "dp", axis=1, tiled=True),
    )


def masked_scores(query_rot, key_rot, segment_row):
    raw_scores = jnp.einsum(
        "qhd,kd->hqk", query_rot, key_rot, preferred_element_type=jnp.float32
    ) / math.sqrt(HD)
    return jnp.where(allowed_of(segment_row)[None], raw_scores, masked_score)


def attend(query_rot, key_rot, value_rows, segment_row):
    scores = masked_scores(query_rot, key_rot, segment_row)
    row_max = jnp.max(scores, axis=2, keepdims=True)
    log_total = row_max + jnp.log(jnp.sum(jnp.exp(scores - row_max), axis=2, keepdims=True))
    probs_low = jnp.exp(scores - log_total).astype(jnp.bfloat16)
    attn_result = jnp.einsum(
        "hqk,kd->qhd", probs_low, value_rows, preferred_element_type=jnp.float32
    )
    return (attn_result, log_total)


def attend_back(query_rot, key_rot, value_rows, segment_row, log_total, attn_result, grad_context):
    scores = masked_scores(query_rot, key_rot, segment_row)
    attn_probs = jnp.exp(scores - log_total)
    probs_low = attn_probs.astype(jnp.bfloat16)
    grad_probs = jnp.einsum(
        "qhd,kd->hqk", grad_context, value_rows, preferred_element_type=jnp.float32
    )
    row_delta = jnp.sum(grad_context.astype(jnp.float32) * attn_result, axis=2).T[:, :, None]
    grad_scores = (attn_probs * (grad_probs - row_delta)).astype(jnp.bfloat16)
    grad_query_rot = jnp.einsum(
        "hqk,kd->qhd", grad_scores, key_rot, preferred_element_type=jnp.float32
    ) / math.sqrt(HD)
    grad_key_rot = jnp.einsum(
        "hqk,qhd->kd", grad_scores, query_rot, preferred_element_type=jnp.float32
    ) / math.sqrt(HD)
    grad_value = jnp.einsum(
        "hqk,qhd->kd", probs_low, grad_context, preferred_element_type=jnp.float32
    )
    return (grad_query_rot, grad_key_rot, grad_value)


def local(
    block_input,
    segment_ids,
    gain_attn,
    w_query,
    b_query,
    w_keyval,
    b_keyval,
    w_out,
    gain_ffn,
    w_gate,
    w_up,
    w_down,
    cotangent,
):
    tensor_index = lax.axis_index("tensor")
    seq_count = segment_ids.shape[0]
    seq_length = segment_ids.shape[1]
    row_count = seq_count * seq_length
    local_heads = b_query.shape[0] // HD
    head_kv = tensor_index * local_heads // (HQ // KV)
    rows_float = block_input.astype(jnp.float32)
    normed_one, scale_one = norm_forward(rows_float)
    act_one = lax.all_gather(
        (normed_one * gain_attn).astype(jnp.bfloat16), "tensor", axis=0, tiled=True
    )
    query_w, keyval_w, out_w = gather_three(w_query, w_keyval, w_out)
    query_rows = matmul(act_one, query_w) + b_query
    keyval = matmul(act_one, keyval_w) + b_keyval
    key_rows = lax.dynamic_slice_in_dim(keyval, head_kv * HD, HD, 1)
    value_rows = lax.dynamic_slice_in_dim(keyval, KV * HD + head_kv * HD, HD, 1).astype(
        jnp.bfloat16
    )
    positions = jax.vmap(positions_of)(segment_ids).reshape(row_count)
    cosine_table, sine_table = rotary(positions)
    cos_heads = cosine_table[:, None, :]
    sin_heads = sine_table[:, None, :]
    query_rot = turn(query_rows.reshape(row_count, local_heads, HD), cos_heads, sin_heads).astype(
        jnp.bfloat16
    )
    key_rot = turn(key_rows, cosine_table, sine_table).astype(jnp.bfloat16)
    query_seq = query_rot.reshape(seq_count, seq_length, local_heads, HD)
    key_seq = key_rot.reshape(seq_count, seq_length, HD)
    value_seq = value_rows.reshape(seq_count, seq_length, HD)
    attn_result, log_total = lax.map(
        lambda seq_items: attend(*seq_items), (query_seq, key_seq, value_seq, segment_ids)
    )
    context = attn_result.astype(jnp.bfloat16).reshape(row_count, local_heads * HD)
    hidden = rows_float + lax.psum_scatter(
        matmul(context, out_w), "tensor", scatter_dimension=0, tiled=True
    )
    normed_two, scale_two = norm_forward(hidden)
    act_two = lax.all_gather(
        (normed_two * gain_ffn).astype(jnp.bfloat16), "tensor", axis=0, tiled=True
    )
    gate_w, up_w, down_w = gather_three(w_gate, w_up, w_down)
    gate_pre = matmul(act_two, gate_w)
    up_part = matmul(act_two, up_w)
    sigmoid_gate = jax.nn.sigmoid(gate_pre)
    silu_gate = gate_pre * sigmoid_gate
    mixed_rows = (silu_gate * up_part).astype(jnp.bfloat16)
    block_out = (
        hidden
        + lax.psum_scatter(
            matmul(mixed_rows, down_w).astype(jnp.bfloat16),
            "tensor",
            scatter_dimension=0,
            tiled=True,
        ).astype(jnp.float32)
    ).astype(jnp.bfloat16)
    cot_rows = lax.all_gather(cotangent, "tensor", axis=0, tiled=True)
    grad_mixed = matmul(cot_rows, down_w.T)
    grad_gate = (
        grad_mixed * up_part * sigmoid_gate * (1.0 + gate_pre * (1.0 - sigmoid_gate))
    ).astype(jnp.bfloat16)
    grad_up = (grad_mixed * silu_gate).astype(jnp.bfloat16)
    grad_gate_w = matmul(act_two.T, grad_gate)
    grad_up_w = matmul(act_two.T, grad_up)
    grad_down_w = matmul(mixed_rows.T, cot_rows)
    grad_act_two = lax.psum_scatter(
        matmul(grad_gate, gate_w.T) + matmul(grad_up, up_w.T),
        "tensor",
        scatter_dimension=0,
        tiled=True,
    )
    back_two, gain_two = norm_backward(grad_act_two, normed_two, scale_two, gain_ffn)
    grad_hidden = cotangent.astype(jnp.float32) + back_two
    grad_attn = lax.all_gather(grad_hidden.astype(jnp.bfloat16), "tensor", axis=0, tiled=True)
    grad_out_w = matmul(context.T, grad_attn)
    grad_context = (
        matmul(grad_attn, out_w.T)
        .astype(jnp.bfloat16)
        .reshape(seq_count, seq_length, local_heads, HD)
    )
    grad_query_rot, grad_key_rot, grad_value = lax.map(
        lambda seq_items: attend_back(*seq_items),
        (query_seq, key_seq, value_seq, segment_ids, log_total, attn_result, grad_context),
    )
    grad_query = turn(
        grad_query_rot.reshape(row_count, local_heads, HD), cos_heads, -sin_heads
    ).reshape(row_count, local_heads * HD)
    grad_key = turn(grad_key_rot.reshape(row_count, HD), cosine_table, -sine_table)
    grad_value = grad_value.reshape(row_count, HD)
    grad_query_low = grad_query.astype(jnp.bfloat16)
    kv_columns = jnp.zeros((row_count, keyval.shape[1]), jnp.bfloat16)
    kv_columns = lax.dynamic_update_slice_in_dim(
        kv_columns, grad_key.astype(jnp.bfloat16), head_kv * HD, 1
    )
    kv_columns = lax.dynamic_update_slice_in_dim(
        kv_columns, grad_value.astype(jnp.bfloat16), KV * HD + head_kv * HD, 1
    )
    bias_keyval = jnp.zeros((keyval.shape[1],), jnp.float32)
    bias_keyval = lax.dynamic_update_slice_in_dim(
        bias_keyval, jnp.sum(grad_key, axis=0), head_kv * HD, 0
    )
    bias_keyval = lax.dynamic_update_slice_in_dim(
        bias_keyval, jnp.sum(grad_value, axis=0), KV * HD + head_kv * HD, 0
    )
    bias_query = lax.dynamic_update_slice_in_dim(
        jnp.zeros((HQ * HD,), jnp.float32),
        jnp.sum(grad_query, axis=0),
        tensor_index * local_heads * HD,
        0,
    )
    grad_query_w = matmul(act_one.T, grad_query_low)
    grad_keyval_w = matmul(act_one.T, kv_columns)
    grad_act_one = lax.psum_scatter(
        (matmul(grad_query_low, query_w.T) + matmul(kv_columns, keyval_w.T)).astype(jnp.bfloat16),
        "tensor",
        scatter_dimension=0,
        tiled=True,
    ).astype(jnp.float32)
    back_one, gain_one = norm_backward(grad_act_one, normed_one, scale_one, gain_attn)
    grad_rows = (grad_hidden + back_one).astype(jnp.bfloat16)
    keyval_share, gain_one_share, gain_two_share, query_bias_share, keyval_bias_share = (
        lax.psum_scatter(grad_keyval_w, ("dp", "tensor"), scatter_dimension=0, tiled=True),
        lax.psum_scatter(gain_one, ("dp", "tensor"), scatter_dimension=0, tiled=True),
        lax.psum_scatter(gain_two, ("dp", "tensor"), scatter_dimension=0, tiled=True),
        lax.psum_scatter(bias_query, ("dp", "tensor"), scatter_dimension=0, tiled=True),
        lax.psum_scatter(bias_keyval, ("dp", "tensor"), scatter_dimension=0, tiled=True),
    )
    query_share, out_share, gate_share, up_share, down_share = (
        lax.psum_scatter(
            grad_query_w.astype(jnp.bfloat16), "dp", scatter_dimension=0, tiled=True
        ).astype(jnp.float32),
        lax.psum_scatter(
            grad_out_w.astype(jnp.bfloat16), "dp", scatter_dimension=1, tiled=True
        ).astype(jnp.float32),
        lax.psum_scatter(
            grad_gate_w.astype(jnp.bfloat16), "dp", scatter_dimension=0, tiled=True
        ).astype(jnp.float32),
        lax.psum_scatter(
            grad_up_w.astype(jnp.bfloat16), "dp", scatter_dimension=0, tiled=True
        ).astype(jnp.float32),
        lax.psum_scatter(
            grad_down_w.astype(jnp.bfloat16), "dp", scatter_dimension=1, tiled=True
        ).astype(jnp.float32),
    )
    return (
        block_out,
        grad_rows,
        gain_one_share,
        query_share,
        query_bias_share,
        keyval_share,
        keyval_bias_share,
        out_share,
        gain_two_share,
        gate_share,
        up_share,
        down_share,
    )


def solution(mesh):
    placed = (
        P(("dp", "tensor"), None),
        P("dp", None),
        P(),
        P("dp", "tensor"),
        P("tensor"),
        P("dp", None),
        P(),
        P("tensor", "dp"),
        P(),
        P("dp", "tensor"),
        P("dp", "tensor"),
        P("tensor", "dp"),
        P(("dp", "tensor"), None),
    )
    return jax.shard_map(
        local,
        mesh=mesh,
        in_specs=placed,
        out_specs=(
            P(("dp", "tensor"), None),
            P(("dp", "tensor"), None),
            P(("dp", "tensor")),
            P("dp", "tensor"),
            P(("dp", "tensor")),
            P(("dp", "tensor"), None),
            P(("dp", "tensor")),
            P("tensor", "dp"),
            P(("dp", "tensor")),
            P("dp", "tensor"),
            P("dp", "tensor"),
            P("tensor", "dp"),
        ),
        check_vma=False,
    )
```

profile of v0, /device:TPU:0, one launch (start us, length us, event | category | flops | bytes accessed | tf_op | source)
XLA Modules:
  0.0 1482.0 jit_solution(15097303568250098657)
XLA Ops:
  14.6 39.4 %all-gather.15.cloned.1.call-done = bf16[1536,384]{1,0:T(8,128)(2,1)} async-done(((bf16[192,384]{1,0:T(8,128)(2,1)}), bf16[1536,384]{1,0:T(8,128)(2,1)}) %all-gather.15.cloned.1.call-update) | async-done | bytes 1179664 | tf_op jit(solution)/shard_map/all_gather | solution.py:62
  54.0 29.5 %all-gather.11.cloned.1.call-done = bf16[1024,1536]{1,0:T(8,128)(2,1)} async-done(((bf16[256,1536]{1,0:T(8,128)(2,1)}), bf16[1024,1536]{1,0:T(8,128)(2,1)}) %all-gather.11.cloned.1.call-update) | async-done | bytes 3145744 | tf_op jit(solution)/shard_map/all_gather | solution.py:130
  88.2 41.7 %all-gather.13.cloned.1.call-done = bf16[1536,512]{1,0:T(8,128)(2,1)} async-done(((bf16[192,512]{1,0:T(8,128)(2,1)}), bf16[1536,512]{1,0:T(8,128)(2,1)}) %all-gather.13.cloned.1.call-update) | async-done | bytes 1572880 | tf_op jit(solution)/shard_map/all_gather | solution.py:63
  144.9 7.3 exponential_reduce_fusion
  152.2 9.5 bitcast_convert_fusion
  161.7 10.1 all-gather.17.cloned.1.call-done
  178.2 56.6 %reduce-scatter.11.cloned.1.call-done = f32[256,1536]{1,0:T(8,128)} async-done(((f32[1024,1536]{1,0:T(8,128)}), f32[256,1536]{1,0:T(8,128)}) %reduce-scatter.11.cloned.1.call-update) | async-done | bytes 1572880 | tf_op jit(solution)/shard_map/reduce_scatter | solution.py:155
  239.8 106.2 %all-gather.21.cloned.1.call-done = bf16[1536,2240]{1,0:T(8,128)(2,1)} async-done(((bf16[192,2240]{1,0:T(8,128)(2,1)}), bf16[1536,2240]{1,0:T(8,128)(2,1)}) %all-gather.21.cloned.1.call-update) | async-done | bytes 6881296 | tf_op jit(solution)/shard_map/all_gather | solution.py:62
  346.0 29.0 %all-gather.19.cloned.1.call-done = bf16[1024,1536]{1,0:T(8,128)(2,1)} async-done(((bf16[256,1536]{1,0:T(8,128)(2,1)}), bf16[1024,1536]{1,0:T(8,128)(2,1)}) %all-gather.19.cloned.1.call-update) | async-done | bytes 3145744 | tf_op jit(solution)/shard_map/all_gather | solution.py:159
  374.9 13.3 fusion.47
  388.3 97.9 %all-gather.23.cloned.1.call-done = bf16[1536,2240]{1,0:T(8,128)(2,1)} async-done(((bf16[192,2240]{1,0:T(8,128)(2,1)}), bf16[1536,2240]{1,0:T(8,128)(2,1)}) %all-gather.23.cloned.1.call-update) | async-done | bytes 6881296 | tf_op jit(solution)/shard_map/all_gather | solution.py:63
  486.2 13.2 fusion.48
  499.4 15.2 %all-gather.27.cloned.1.call-done = bf16[1024,1536]{1,0:T(8,128)(2,1)} async-done(((bf16[256,1536]{1,0:T(8,128)(2,1)}), bf16[1024,1536]{1,0:T(8,128)(2,1)}) %all-gather.27.cloned.1.call-update) | async-done | bytes 3145744 | tf_op jit(solution)/shard_map/all_gather | solution.py:177
  514.6 111.1 %all-gather.25.cloned.1.call-done = bf16[2240,1536]{0,1:T(8,128)(2,1)} async-done(((bf16[2240,192]{0,1:T(8,128)(2,1)}), bf16[2240,1536]{0,1:T(8,128)(2,1)}) %all-gather.25.cloned.1.call-update) | async-done | bytes 6881296 | tf_op jit(solution)/shard_map/all_gather | solution.py:64
  625.7 20.2 %multiply_convert_fusion = (bf16[1024,2240]{0,1:T(8,128)(2,1)}, bf16[1024,2240]{0,1:T(8,128)(2,1)}, bf16[1024,2240]{0,1:T(8,128)(2,1)}) fusion(f32[1024,2240]{0,1:T(8,128)} %fusion.47, f32[1024,2240]{0,1:T(8,128)} %fusion.48, bf16[1024,1536]{1,0:T(8,128)(2,1)} %all-gather.27.cloned.1.call-done, bf16[2240,1536]{0,1:T(8,128)(2,1)} %all-gather.25.cloned.1.call-done), kind=kOutput, calls=%fused_computation.10 | convolution fusion | flops 7080837120 | bytes 42139648 | tf_op jit(solution)/shard_map/dot_general | solution.py:16
  645.8 11.4 fusion.49
  657.3 10.1 convolution_add_fusion
  667.4 56.6 %reduce-scatter.15.cloned.1.call-done = f32[256,1536]{1,0:T(8,128)} async-done(((f32[1024,1536]{1,0:T(8,128)}), f32[256,1536]{1,0:T(8,128)}) %reduce-scatter.15.cloned.1.call-update) | async-done | bytes 1572880 | tf_op jit(solution)/shard_map/reduce_scatter | solution.py:186
  727.5 12.3 convolution_convert_fusion.2
  739.9 12.6 convolution_convert_fusion.1
  752.6 12.4 convolution_convert_fusion
  773.4 9.4 fusion.1
  791.3 9.1 fusion.45
  816.0 12.5 convolution_convert_fusion.3
  835.2 53.8 %reduce-scatter.25.cloned.1.call-done = bf16[192,2240]{1,0:T(8,128)(2,1)} async-done(((bf16[1536,2240]{1,0:T(8,128)(2,1)}), bf16[192,2240]{1,0:T(8,128)(2,1)}) %reduce-scatter.25.cloned.1.call-update) | async-done | bytes 860176 | tf_op jit(solution)/shard_map/reduce_scatter | solution.py:255
  891.4 129.6 %reduce-scatter.27.cloned.1.call-done = bf16[192,2240]{1,0:T(8,128)(2,1)} async-done(((bf16[1536,2240]{1,0:T(8,128)(2,1)}), bf16[192,2240]{1,0:T(8,128)(2,1)}) %reduce-scatter.27.cloned.1.call-update) | async-done | bytes 860176 | tf_op jit(solution)/shard_map/reduce_scatter | solution.py:258
  1023.5 129.1 %reduce-scatter.29.cloned.1.call-done = bf16[2240,192]{0,1:T(8,128)(2,1)} async-done(((bf16[2240,1536]{0,1:T(8,128)(2,1)}), bf16[2240,192]{0,1:T(8,128)(2,1)}) %reduce-scatter.29.cloned.1.call-update) | async-done | bytes 860176 | tf_op jit(solution)/shard_map/reduce_scatter | solution.py:261
  1155.6 63.8 %reduce-scatter.23.cloned.1.call-done = bf16[384,192]{0,1:T(8,128)(2,1)} async-done(((bf16[384,1536]{0,1:T(8,128)(2,1)}), bf16[384,192]{0,1:T(8,128)(2,1)}) %reduce-scatter.23.cloned.1.call-update) | async-done | bytes 147472 | tf_op jit(solution)/shard_map/reduce_scatter | solution.py:252
  1221.0 65.0 %reduce-scatter.19.cloned.1.call-done = bf16[192,384]{1,0:T(8,128)(2,1)} async-done(((bf16[1536,384]{1,0:T(8,128)(2,1)}), bf16[192,384]{1,0:T(8,128)(2,1)}) %reduce-scatter.19.cloned.1.call-update) | async-done | bytes 147472 | tf_op jit(solution)/shard_map/reduce_scatter | solution.py:249
  1287.6 37.9 %reduce-scatter.17.cloned.1.call-done = bf16[256,1536]{1,0:T(8,128)(2,1)} async-done(((bf16[1024,1536]{1,0:T(8,128)(2,1)}), bf16[256,1536]{1,0:T(8,128)(2,1)}) %reduce-scatter.17.cloned.1.call-update) | async-done | bytes 786448 | tf_op jit(solution)/shard_map/reduce_scatter | solution.py:233
  1327.4 39.9 %all-reduce.4 = (f32[1536]{0:T(1024)S(1)}, f32[1536]{0:T(1024)S(1)}, f32[512]{0:T(512)S(1)}, f32[1536]{0:T(1024)S(1)}) all-reduce(f32[1536]{0:T(1024)S(1)} %get-tuple-element.57, f32[1536]{0:T(1024)S(1)} %bitcast_dynamic-update-slice_fusion, ...), channel_id=6, replica_groups=mesh['dp'=8,'tensor'=4] {'dp','tensor'}, use_global_device_ids=true, to_apply=%region_14.15.clone | all-reduce | flops 5120 | bytes 40960
  1373.4 101.5 %reduce-scatter.21.cloned.1.call-done = f32[48,512]{1,0:T(8,128)} async-done(((f32[1536,512]{1,0:T(8,128)}), f32[48,512]{1,0:T(8,128)}) %reduce-scatter.21.cloned.1.call-update) | async-done | bytes 98320 | tf_op jit(solution)/shard_map/reduce_scatter | solution.py:242
  (175 shorter events, 99.8 us)
Async XLA Ops:
  7.2 76.3 %copy-start.32 = (f32[384]{0:T(512)S(1)}, f32[384]{0:T(512)}, u32[]{:S(2)}) copy-start(f32[384]{0:T(512)} %param.17) | copy-start | bytes 4612
  7.2 46.8 %all-gather.15.cloned.1.call-start = ((), (), s32[]{:S(2)}) async-start(), calls=%async_computation.12 | async-start | bytes 1327104 | tf_op jit(solution)/shard_map/all_gather | solution.py:62
  7.9 75.5 %all-gather.11.cloned.1.call-start = ((), (), s32[]{:S(2)}) async-start(), calls=%async_computation.10 | async-start | bytes 3932160 | tf_op jit(solution)/shard_map/all_gather | solution.py:130
  11.7 118.2 %all-gather.13.cloned.1.call-start = ((), (), s32[]{:S(2)}) async-start(), calls=%async_computation.11 | async-start | bytes 1769472 | tf_op jit(solution)/shard_map/all_gather | solution.py:63
  12.4 159.4 %all-gather.17.cloned.1.call-start = ((), (), s32[]{:S(2)}) async-start(), calls=%async_computation.13 | async-start | bytes 1327104 | tf_op jit(solution)/shard_map/all_gather | solution.py:64
  13.0 221.9 %reduce-scatter.11.cloned.1.call-start = ((), (), s32[]{:S(2)}) async-start(), calls=%async_computation.14 | async-start | bytes 7864320 | tf_op jit(solution)/shard_map/reduce_scatter | solution.py:155
  87.1 42.8 %copy-start.33 = (f32[512]{0:T(512)S(1)}, f32[512]{0:T(512)}, u32[]{:S(2)}) copy-start(f32[512]{0:T(512)} %param.19) | copy-start | bytes 6148
  134.1 18.1 %copy-start.22 = (f32[1024,512]{0,1:T(8,128)}, f32[1024,512]{0,1:T(8,128)S(1)}, u32[]{:S(2)}) copy-start(f32[1024,512]{0,1:T(8,128)S(1)} %convolution_add_fusion.1) | copy-start | bytes 6291460
  161.7 15.8 %copy-start.13 = (bf16[1024,3,128]{0,2,1:T(8,128)(2,1)}, bf16[1024,3,128]{0,2,1:T(8,128)(2,1)S(1)}, u32[]{:S(2)}) copy-start(bf16[1024,3,128]{0,2,1:T(8,128)(2,1)S(1)} %get-tuple-element.102) | copy-start | bytes 2359300
  177.5 57.3 %copy-start = (bf16[256,1536]{1,0:T(8,128)(2,1)S(1)}, bf16[256,1536]{1,0:T(8,128)(2,1)}, u32[]{:S(2)}) copy-start(bf16[256,1536]{1,0:T(8,128)(2,1)} %param.13) | copy-start | bytes 2359300
  177.6 59.0 %copy-start.23 = (f32[1536]{0:T(1024)S(1)}, f32[1536]{0:T(1024)}, u32[]{:S(2)}) copy-start(f32[1536]{0:T(1024)} %param.21) | copy-start | bytes 18436
  177.6 168.4 %all-gather.21.cloned.1.call-start = ((), (), s32[]{:S(2)}) async-start(), calls=%async_computation.16 | async-start | bytes 7962624 | tf_op jit(solution)/shard_map/all_gather | solution.py:62
  178.2 196.8 %all-gather.19.cloned.1.call-start = ((), (), s32[]{:S(2)}) async-start(), calls=%async_computation.15 | async-start | bytes 3932160 | tf_op jit(solution)/shard_map/all_gather | solution.py:159
  237.7 248.5 %all-gather.23.cloned.1.call-start = ((), (), s32[]{:S(2)}) async-start(), calls=%async_computation.17 | async-start | bytes 7962624 | tf_op jit(solution)/shard_map/all_gather | solution.py:63
  238.4 276.1 %all-gather.27.cloned.1.call-start = ((), (), s32[]{:S(2)}) async-start(), calls=%async_computation.20 | async-start | bytes 3932160 | tf_op jit(solution)/shard_map/all_gather | solution.py:177
  239.1 386.5 %all-gather.25.cloned.1.call-start = ((), (), s32[]{:S(2)}) async-start(), calls=%async_computation.18 | async-start | bytes 7962624 | tf_op jit(solution)/shard_map/all_gather | solution.py:64
  239.7 484.3 %reduce-scatter.15.cloned.1.call-start = ((), (), s32[]{:S(2)}) async-start(), calls=%async_computation.21 | async-start | bytes 7864320 | tf_op jit(solution)/shard_map/reduce_scatter | solution.py:186
  645.8 11.4 copy-start.28
  645.8 11.4 copy-start.34
  667.4 58.7 %copy-start.3 = (bf16[256,1536]{1,0:T(8,128)(2,1)S(1)}, bf16[256,1536]{1,0:T(8,128)(2,1)}, u32[]{:S(2)}) copy-start(bf16[256,1536]{1,0:T(8,128)(2,1)} %param.25) | copy-start | bytes 2359300
  667.4 97.7 %all-gather.29.cloned.1.call-start = ((), (), s32[]{:S(2)}) async-start(), calls=%async_computation.22 | async-start | bytes 3932160 | tf_op jit(solution)/shard_map/all_gather | solution.py:194
  727.5 161.4 %reduce-scatter.25.cloned.1.call-start = ((), (), s32[]{:S(2)}) async-start(), calls=%async_computation.27 | async-start | bytes 7962624 | tf_op jit(solution)/shard_map/reduce_scatter | solution.py:255
  739.9 281.1 %reduce-scatter.27.cloned.1.call-start = ((), (), s32[]{:S(2)}) async-start(), calls=%async_computation.28 | async-start | bytes 7962624 | tf_op jit(solution)/shard_map/reduce_scatter | solution.py:258
  752.6 400.0 %reduce-scatter.29.cloned.1.call-start = ((), (), s32[]{:S(2)}) async-start(), calls=%async_computation.29 | async-start | bytes 7962624 | tf_op jit(solution)/shard_map/reduce_scatter | solution.py:261
  765.0 454.3 %reduce-scatter.23.cloned.1.call-start = ((), (), s32[]{:S(2)}) async-start(), calls=%async_computation.26 | async-start | bytes 1327104 | tf_op jit(solution)/shard_map/reduce_scatter | solution.py:252
  773.2 512.8 %reduce-scatter.19.cloned.1.call-start = ((), (), s32[]{:S(2)}) async-start(), calls=%async_computation.24 | async-start | bytes 1327104 | tf_op jit(solution)/shard_map/reduce_scatter | solution.py:249
  790.9 534.7 %reduce-scatter.17.cloned.1.call-start = ((), (), s32[]{:S(2)}) async-start(), calls=%async_computation.23 | async-start | bytes 3932160 | tf_op jit(solution)/shard_map/reduce_scatter | solution.py:233
  815.8 553.8 %reduce-scatter.13.cloned.1.call-start = ((), (), s32[]{:S(2)}) async-start(), calls=%async_computation.19 | async-start | bytes 3932160 | tf_op jit(solution)/shard_map/reduce_scatter | solution.py:170
  828.6 646.4 %reduce-scatter.21.cloned.1.call-start = ((), (), s32[]{:S(2)}) async-start(), calls=%async_computation.25 | async-start | bytes 3244032 | tf_op jit(solution)/shard_map/reduce_scatter | solution.py:242
  891.4 434.2 %copy-start.1 = (bf16[256,1536]{1,0:T(8,128)(2,1)S(1)}, bf16[256,1536]{1,0:T(8,128)(2,1)}, u32[]{:S(2)}) copy-start(bf16[256,1536]{1,0:T(8,128)(2,1)} %param.13) | copy-start | bytes 2359300
  891.4 434.2 %copy-start.24 = (f32[1536]{0:T(1024)S(1)}, f32[1536]{0:T(1024)}, u32[]{:S(2)}) copy-start(f32[1536]{0:T(1024)} %param.15) | copy-start | bytes 18436
  891.4 434.2 %copy-start.27 = (f32[256]{0:T(256)S(1)}, f32[256]{0:T(256)}, u32[]{:S(2)}) copy-start(f32[256]{0:T(256)} %copy-done.26) | copy-start | bytes 3076
  (23 other events, 76.9 us)
Sparse Core Ops, SparseCore 0:
  10.2 43.7 all-gather.14
  56.1 27.2 all-gather.10
  85.7 44.1 all-gather.12
  131.9 39.8 all-gather.16
  177.7 57.1 reduce-scatter.10
  237.1 108.7 all-gather.20
  348.2 26.7 all-gather.18
  377.3 108.7 all-gather.22
  487.8 26.7 all-gather.26
  516.8 108.7 all-gather.24
  667.5 56.5 reduce-scatter.14
  727.6 28.5 all-gather.28
  759.9 129.0 reduce-scatter.24
  892.9 128.0 reduce-scatter.26
  1024.5 128.0 reduce-scatter.28
  1156.2 63.0 reduce-scatter.22
  1222.9 62.9 reduce-scatter.18
  1288.5 36.9 reduce-scatter.16
  1328.1 38.3 reduce-scatter.12
  1373.2 101.6 reduce-scatter.20
where the time goes:
time: 1490 us; the launch traced here: 1480 us
  waiting for transfers between devices  1180 us (79%)
  matrix products  193 us (13%)
  other arithmetic  42.9 us (3%)
  blocking collectives  39.9 us (3%)
  between operations  15.1 us (1%)
    dot_general x18, matrix products, matmul(): return jnp.dot(left, right, preferred_element_type=jnp.float32)  152 us
    all_gather x2, waiting for transfers between devices, gather_three(): lax.all_gather(first, 'dp', axis=0, tiled=True)  146 us
    all_gather x2, waiting for transfers between devices, gather_three(): lax.all_gather(second, 'dp', axis=0, tiled=True)  140 us
    reduce_scatter x1, waiting for transfers between devices, local(): lax.psum_scatter(grad_up_w.astype(jnp.bfloat16), 'dp', scatter_dimension=...  130 us
    reduce_scatter x1, waiting for transfers between devices, local(): lax.psum_scatter(grad_down_w.astype(jnp.bfloat16), 'dp', scatter_dimensio...  129 us
    all_gather x2, waiting for transfers between devices, gather_three(): lax.all_gather(third, 'dp', axis=1, tiled=True)  121 us
    reduce_scatter x1, waiting for transfers between devices, local(): lax.psum_scatter(grad_keyval_w, ('dp', 'tensor'), scatter_dimension=0, ti...  101 us
    reduce_scatter x1, waiting for transfers between devices, local(): lax.psum_scatter(grad_query_w.astype(jnp.bfloat16), 'dp', scatter_dimensi...  65 us
  transfers between devices with their start and end apart: 20, of which 18 were waited for; matrix products, arithmetic and copies ran while one was open for 13% of the time, Pallas kernels for 0%

commit v1 on v0

--- a/solution.py
+++ b/solution.py
@@ -12,6 +12,19 @@
 masked_score = -1e30
 
 
+def ring_gather(x, axis, dim):
+    size, position, extent = (lax.axis_size(axis), lax.axis_index(axis), x.shape[dim])
+    upward = [(i, (i + 1) % size) for i in range(size)]
+    result = jnp.zeros((*x.shape[:dim], size * extent, *x.shape[dim + 1 :]), x.dtype)
+    held = x
+    for step in range(size):
+        source = (position - step) % size
+        result = lax.dynamic_update_slice_in_dim(result, held, source * extent, axis=dim)
+        if step < size - 1:
+            held = lax.ppermute(held, axis, upward)
+    return result
+
+
 def matmul(left, right):
     return jnp.dot(left, right, preferred_element_type=jnp.float32)
 
@@ -59,7 +72,7 @@
 
 def gather_three(first, second, third):
     return (
-        lax.all_gather(first, "dp", axis=0, tiled=True),
+        ring_gather(first, "dp", 0),
         lax.all_gather(second, "dp", axis=0, tiled=True),
         lax.all_gather(third, "dp", axis=1, tiled=True),
     )

time: 1490 us -> 1390 us (0.933)
  waiting for transfers between devices: 1180 us -> 1070 us
  local copies, waits for them, and re-layouts: 11.4 us -> 29.2 us
    ppermute x0 -> x14, waiting for transfers between devices: none -> 233 us  [ring_gather(): held = lax.ppermute(held, axis, upward)]
    all_gather x2 -> x0, waiting for transfers between devices: 146 us -> none  [gather_three(): lax.all_gather(first, 'dp', axis=0, tiled=True)]
    reduce_scatter x1, waiting for transfers between devices: 53.8 us -> 130 us  [local(): lax.psum_scatter(grad_gate_w.astype(jnp.bfloat16), 'dp', scatter_dimensio...]
    reduce_scatter x1, waiting for transfers between devices: 130 us -> 53.8 us  [local(): lax.psum_scatter(grad_up_w.astype(jnp.bfloat16), 'dp', scatter_dimension=...]
    all_gather x2, waiting for transfers between devices: 121 us -> 53.6 us  [gather_three(): lax.all_gather(third, 'dp', axis=1, tiled=True)]
    reduce_scatter x1, waiting for transfers between devices: 56.6 us -> 0.01 us  [local(): lax.psum_scatter(matmul(context, out_w), 'tensor', scatter_dimension=0, t...]
    all_gather x1, waiting for transfers between devices: 29.5 us -> 0.02 us  [local(): lax.all_gather((normed_one * gain_attn).astype(jnp.bfloat16), 'tensor', a...]
    all_gather x2, waiting for transfers between devices: 140 us -> 111 us  [gather_three(): lax.all_gather(second, 'dp', axis=0, tiled=True)]
  transfers between devices with their start and end apart: 20 -> 32, of which waited for: 18 -> 27; matrix products, arithmetic and copies ran while one was open for 13% -> 13% of each run, Pallas kernels for 0% -> 0%
where the time goes in v1:
time: 1390 us
  waiting for transfers between devices  1070 us (77%)
  matrix products  188 us (14%)
  other arithmetic  40 us (3%)
  blocking collectives  39.9 us (3%)
  local copies, waits for them, and re-layouts  29.2 us (2%)
  between operations  15.6 us (1%)
    ppermute x14, waiting for transfers between devices, ring_gather(): held = lax.ppermute(held, axis, upward)  233 us
    dot_general x18, matrix products, matmul(): return jnp.dot(left, right, preferred_element_type=jnp.float32)  157 us
    reduce_scatter x1, waiting for transfers between devices, local(): lax.psum_scatter(grad_gate_w.astype(jnp.bfloat16), 'dp', scatter_dimensio...  130 us
    reduce_scatter x1, waiting for transfers between devices, local(): lax.psum_scatter(grad_down_w.astype(jnp.bfloat16), 'dp', scatter_dimensio...  129 us
    all_gather x2, waiting for transfers between devices, gather_three(): lax.all_gather(second, 'dp', axis=0, tiled=True)  111 us
    reduce_scatter x1, waiting for transfers between devices, local(): lax.psum_scatter(grad_keyval_w, ('dp', 'tensor'), scatter_dimension=0, ti...  101 us
    reduce_scatter x1, waiting for transfers between devices, local(): lax.psum_scatter(grad_query_w.astype(jnp.bfloat16), 'dp', scatter_dimensi...  65 us
    reduce_scatter x1, waiting for transfers between devices, local(): lax.psum_scatter(grad_out_w.astype(jnp.bfloat16), 'dp', scatter_dimension...  63.8 us
  transfers between devices with their start and end apart: 32, of which 27 were waited for; matrix products, arithmetic and copies ran while one was open for 13% of the time, Pallas kernels for 0%

profile of v1, /device:TPU:0, one launch (start us, length us, event | category | flops | bytes accessed | tf_op | source)
XLA Modules:
  0.0 1386.9 jit_solution(11749077130635578973)
XLA Ops:
  53.1 11.9 collective-permute-done.5
  77.3 13.3 all-gather.11.cloned.1.call-done
  113.3 19.4 %all-gather.13.cloned.1.call-done = bf16[384,1536]{0,1:T(8,128)(2,1)} async-done(((bf16[384,192]{0,1:T(8,128)(2,1)}), bf16[384,1536]{0,1:T(8,128)(2,1)}) %all-gather.13.cloned.1.call-update) | async-done | bytes 1179664 | tf_op jit(solution)/shard_map/all_gather | solution.py:77
  141.3 22.3 %collective-permute-done.7 = bf16[192,2240]{1,0:T(8,128)(2,1)S(1)} collective-permute-done((bf16[192,2240]{1,0:T(8,128)(2,1)S(1)}, bf16[192,2240]{1,0:T(8,128)(2,1)S(1)}, u32[]{:S(2)}, u32[]{:S(2)}) %collective-permute-start.7) | collective-permute-done | bytes 860192 | tf_op jit(solution)/shard_map/ppermute | solution.py:24
  164.5 21.9 %collective-permute-done.8 = bf16[192,2240]{1,0:T(8,128)(2,1)S(1)} collective-permute-done((bf16[192,2240]{1,0:T(8,128)(2,1)S(1)}, bf16[192,2240]{1,0:T(8,128)(2,1)S(1)}, u32[]{:S(2)}, u32[]{:S(2)}) %collective-permute-start.8) | collective-permute-done | bytes 860192 | tf_op jit(solution)/shard_map/ppermute | solution.py:24
  187.5 21.0 %collective-permute-done.9 = bf16[192,2240]{1,0:T(8,128)(2,1)S(1)} collective-permute-done((bf16[192,2240]{1,0:T(8,128)(2,1)S(1)}, bf16[192,2240]{1,0:T(8,128)(2,1)S(1)}, u32[]{:S(2)}, u32[]{:S(2)}) %collective-permute-start.9) | collective-permute-done | bytes 860192 | tf_op jit(solution)/shard_map/ppermute | solution.py:24
  209.4 20.2 %collective-permute-done.10 = bf16[192,2240]{1,0:T(8,128)(2,1)} collective-permute-done((bf16[192,2240]{1,0:T(8,128)(2,1)S(1)}, bf16[192,2240]{1,0:T(8,128)(2,1)}, u32[]{:S(2)}, u32[]{:S(2)}) %collective-permute-start.10) | collective-permute-done | bytes 860192 | tf_op jit(solution)/shard_map/ppermute | solution.py:24
  236.8 29.1 %collective-permute-done.11 = bf16[192,2240]{1,0:T(8,128)(2,1)} collective-permute-done((bf16[192,2240]{1,0:T(8,128)(2,1)}, bf16[192,2240]{1,0:T(8,128)(2,1)}, u32[]{:S(2)}, u32[]{:S(2)}) %collective-permute-start.11) | collective-permute-done | bytes 860192 | tf_op jit(solution)/shard_map/ppermute | solution.py:24
  268.8 32.4 %collective-permute-done.12 = bf16[192,2240]{1,0:T(8,128)(2,1)S(1)} collective-permute-done((bf16[192,2240]{1,0:T(8,128)(2,1)}, bf16[192,2240]{1,0:T(8,128)(2,1)S(1)}, u32[]{:S(2)}, u32[]{:S(2)}) %collective-permute-start.12) | collective-permute-done | bytes 860192 | tf_op jit(solution)/shard_map/ppermute | solution.py:24
  306.5 31.7 %collective-permute-done.13 = bf16[192,2240]{1,0:T(8,128)(2,1)S(1)} collective-permute-done((bf16[192,2240]{1,0:T(8,128)(2,1)S(1)}, bf16[192,2240]{1,0:T(8,128)(2,1)S(1)}, u32[]{:S(2)}, u32[]{:S(2)}) %collective-permute-start.13) | collective-permute-done | bytes 860192 | tf_op jit(solution)/shard_map/ppermute | solution.py:24
  339.2 34.2 %all-gather.19.cloned.1.call-done = bf16[2240,1536]{0,1:T(8,128)(2,1)} async-done(((bf16[2240,192]{0,1:T(8,128)(2,1)}), bf16[2240,1536]{0,1:T(8,128)(2,1)}) %all-gather.19.cloned.1.call-update) | async-done | bytes 6881296 | tf_op jit(solution)/shard_map/all_gather | solution.py:77
  373.4 13.2 fusion.48
  386.6 97.5 %all-gather.17.cloned.1.call-done = bf16[1536,2240]{1,0:T(8,128)(2,1)} async-done(((bf16[192,2240]{1,0:T(8,128)(2,1)}), bf16[1536,2240]{1,0:T(8,128)(2,1)}) %all-gather.17.cloned.1.call-update) | async-done | bytes 6881296 | tf_op jit(solution)/shard_map/all_gather | solution.py:76
  484.1 29.0 %all-gather.15.cloned.1.call-done = bf16[1024,1536]{1,0:T(8,128)(2,1)} async-done(((bf16[256,1536]{1,0:T(8,128)(2,1)}), bf16[1024,1536]{1,0:T(8,128)(2,1)}) %all-gather.15.cloned.1.call-update) | async-done | bytes 3145744 | tf_op jit(solution)/shard_map/all_gather | solution.py:172
  513.1 13.2 fusion.47
  526.3 20.4 %multiply_convert_fusion.1 = (bf16[1024,2240]{0,1:T(8,128)(2,1)}, bf16[1024,2240]{0,1:T(8,128)(2,1)}, bf16[1024,2240]{0,1:T(8,128)(2,1)}) fusion(f32[1024,2240]{0,1:T(8,128)} %fusion.48, f32[1024,2240]{0,1:T(8,128)} %fusion.47, bf16[1024,1536]{1,0:T(8,128)(2,1)} %all-gather.15.cloned.1.call-done, bf16[1536,2240]{1,0:T(8,128)(2,1)} %constant_dynamic-update-slice_fusion.1), kind=kOutput, calls=%fused_computation.11 | convolution fusion | flops 7080837120 | bytes 42139648 | tf_op jit(solution)/shard_map/dot_general | solution.py:29
  546.7 11.4 fusion.49
  558.1 12.1 convolution_add_fusion
  570.3 58.5 %reduce-scatter.15.cloned.1.call-done = f32[256,1536]{1,0:T(8,128)} async-done(((f32[1024,1536]{1,0:T(8,128)}), f32[256,1536]{1,0:T(8,128)}) %reduce-scatter.15.cloned.1.call-update) | async-done | bytes 1572880 | tf_op jit(solution)/shard_map/reduce_scatter | solution.py:199
  632.2 12.3 convolution_convert_fusion.1
  644.6 12.6 convolution_convert_fusion.2
  657.3 12.4 convolution_convert_fusion
  695.8 9.0 fusion.45
  720.6 12.5 convolution_convert_fusion.3
  739.8 53.8 %reduce-scatter.27.cloned.1.call-done = bf16[192,2240]{1,0:T(8,128)(2,1)} async-done(((bf16[1536,2240]{1,0:T(8,128)(2,1)}), bf16[192,2240]{1,0:T(8,128)(2,1)}) %reduce-scatter.27.cloned.1.call-update) | async-done | bytes 860176 | tf_op jit(solution)/shard_map/reduce_scatter | solution.py:271
  796.1 129.6 %reduce-scatter.25.cloned.1.call-done = bf16[192,2240]{1,0:T(8,128)(2,1)} async-done(((bf16[1536,2240]{1,0:T(8,128)(2,1)}), bf16[192,2240]{1,0:T(8,128)(2,1)}) %reduce-scatter.25.cloned.1.call-update) | async-done | bytes 860176 | tf_op jit(solution)/shard_map/reduce_scatter | solution.py:268
  928.2 129.3 %reduce-scatter.29.cloned.1.call-done = bf16[2240,192]{0,1:T(8,128)(2,1)} async-done(((bf16[2240,1536]{0,1:T(8,128)(2,1)}), bf16[2240,192]{0,1:T(8,128)(2,1)}) %reduce-scatter.29.cloned.1.call-update) | async-done | bytes 860176 | tf_op jit(solution)/shard_map/reduce_scatter | solution.py:274
  1060.4 63.8 %reduce-scatter.23.cloned.1.call-done = bf16[384,192]{0,1:T(8,128)(2,1)} async-done(((bf16[384,1536]{0,1:T(8,128)(2,1)}), bf16[384,192]{0,1:T(8,128)(2,1)}) %reduce-scatter.23.cloned.1.call-update) | async-done | bytes 147472 | tf_op jit(solution)/shard_map/reduce_scatter | solution.py:265
  1125.9 65.0 %reduce-scatter.19.cloned.1.call-done = bf16[192,384]{1,0:T(8,128)(2,1)} async-done(((bf16[1536,384]{1,0:T(8,128)(2,1)}), bf16[192,384]{1,0:T(8,128)(2,1)}) %reduce-scatter.19.cloned.1.call-update) | async-done | bytes 147472 | tf_op jit(solution)/shard_map/reduce_scatter | solution.py:262
  1192.5 37.9 %reduce-scatter.17.cloned.1.call-done = bf16[256,1536]{1,0:T(8,128)(2,1)} async-done(((bf16[1024,1536]{1,0:T(8,128)(2,1)}), bf16[256,1536]{1,0:T(8,128)(2,1)}) %reduce-scatter.17.cloned.1.call-update) | async-done | bytes 786448 | tf_op jit(solution)/shard_map/reduce_scatter | solution.py:246
  1232.2 39.9 %all-reduce.4 = (f32[1536]{0:T(1024)S(1)}, f32[1536]{0:T(1024)S(1)}, f32[512]{0:T(512)S(1)}, f32[1536]{0:T(1024)S(1)}) all-reduce(f32[1536]{0:T(1024)S(1)} %get-tuple-element.57, f32[1536]{0:T(1024)S(1)} %bitcast_dynamic-update-slice_fusion, ...), channel_id=6, replica_groups=mesh['dp'=8,'tensor'=4] {'dp','tensor'}, use_global_device_ids=true, to_apply=%region_14.15.clone | all-reduce | flops 5120 | bytes 40960
  1278.3 101.3 %reduce-scatter.21.cloned.1.call-done = f32[48,512]{1,0:T(8,128)} async-done(((f32[1536,512]{1,0:T(8,128)}), f32[48,512]{1,0:T(8,128)}) %reduce-scatter.21.cloned.1.call-update) | async-done | bytes 98320 | tf_op jit(solution)/shard_map/reduce_scatter | solution.py:255
  (235 shorter events, 179.2 us)
Async XLA Ops:
  7.2 66.1 %all-gather.9.cloned.1.call-start = ((), (), s32[]{:S(2)}) async-start(), calls=%async_computation.10 | async-start | bytes 3932160 | tf_op jit(solution)/shard_map/all_gather | solution.py:143
  10.9 79.7 %all-gather.11.cloned.1.call-start = ((), (), s32[]{:S(2)}) async-start(), calls=%async_computation.11 | async-start | bytes 1769472 | tf_op jit(solution)/shard_map/all_gather | solution.py:76
  11.7 121.0 %all-gather.13.cloned.1.call-start = ((), (), s32[]{:S(2)}) async-start(), calls=%async_computation.12 | async-start | bytes 1327104 | tf_op jit(solution)/shard_map/all_gather | solution.py:77
  11.8 9.9 collective-permute-start
  14.8 214.8 %reduce-scatter.11.cloned.1.call-start = ((), (), s32[]{:S(2)}) async-start(), calls=%async_computation.13 | async-start | bytes 7864320 | tf_op jit(solution)/shard_map/reduce_scatter | solution.py:168
  21.7 7.8 collective-permute-start.1
  29.5 7.8 collective-permute-start.2
  37.3 7.8 collective-permute-start.3
  45.2 7.8 collective-permute-start.4
  53.0 11.9 collective-permute-start.5
  65.0 8.3 collective-permute-start.6
  138.7 200.5 %all-gather.21.cloned.1.call-start = ((), (), s32[]{:S(2)}) async-start(), calls=%async_computation.18 | async-start | bytes 3932160 | tf_op jit(solution)/shard_map/all_gather | solution.py:190
  139.3 234.1 %all-gather.19.cloned.1.call-start = ((), (), s32[]{:S(2)}) async-start(), calls=%async_computation.16 | async-start | bytes 7962624 | tf_op jit(solution)/shard_map/all_gather | solution.py:77
  139.9 344.3 %all-gather.17.cloned.1.call-start = ((), (), s32[]{:S(2)}) async-start(), calls=%async_computation.15 | async-start | bytes 7962624 | tf_op jit(solution)/shard_map/all_gather | solution.py:76
  140.6 372.5 %all-gather.15.cloned.1.call-start = ((), (), s32[]{:S(2)}) async-start(), calls=%async_computation.14 | async-start | bytes 3932160 | tf_op jit(solution)/shard_map/all_gather | solution.py:172
  140.7 22.9 %collective-permute-start.7 = (bf16[192,2240]{1,0:T(8,128)(2,1)S(1)}, bf16[192,2240]{1,0:T(8,128)(2,1)S(1)}, u32[]{:S(2)}, u32[]{:S(2)}) collective-permute-start(bf16[192,2240]{1,0:T(8,128)(2,1)S(1)} %copy-done.22), channel_id=1, source_target_pairs={{0,4},{4,8},{8,12},{12,16},{16,20},{20,24},{24,28},{28,0},{1,5},{5... | collective-permute-start | bytes 2580488 | tf_op jit(solution)/shard_map/ppermute | solution.py:24
  164.5 21.9 %collective-permute-start.8 = (bf16[192,2240]{1,0:T(8,128)(2,1)S(1)}, bf16[192,2240]{1,0:T(8,128)(2,1)S(1)}, u32[]{:S(2)}, u32[]{:S(2)}) collective-permute-start(bf16[192,2240]{1,0:T(8,128)(2,1)S(1)} %collective-permute-done.7), channel_id=1, source_target_pairs={{0,4},{4,8},{8,12},{12,16},{16,20},{20,24},{24,28},{28,0},{1,5},{5... | collective-permute-start | bytes 2580488 | tf_op jit(solution)/shard_map/ppermute | solution.py:24
  187.3 21.2 %collective-permute-start.9 = (bf16[192,2240]{1,0:T(8,128)(2,1)S(1)}, bf16[192,2240]{1,0:T(8,128)(2,1)S(1)}, u32[]{:S(2)}, u32[]{:S(2)}) collective-permute-start(bf16[192,2240]{1,0:T(8,128)(2,1)S(1)} %collective-permute-done.8), channel_id=1, source_target_pairs={{0,4},{4,8},{8,12},{12,16},{16,20},{20,24},{24,28},{28,0},{1,5},{5... | collective-permute-start | bytes 2580488 | tf_op jit(solution)/shard_map/ppermute | solution.py:24
  209.4 20.2 %collective-permute-start.10 = (bf16[192,2240]{1,0:T(8,128)(2,1)S(1)}, bf16[192,2240]{1,0:T(8,128)(2,1)}, u32[]{:S(2)}, u32[]{:S(2)}) collective-permute-start(bf16[192,2240]{1,0:T(8,128)(2,1)S(1)} %collective-permute-done.9), channel_id=1, source_target_pairs={{0,4},{4,8},{8,12},{12,16},{16,20},{20,24},{24,28},{28,0},{1,5},{5... | collective-permute-start | bytes 2580488 | tf_op jit(solution)/shard_map/ppermute | solution.py:24
  229.6 36.2 %collective-permute-start.11 = (bf16[192,2240]{1,0:T(8,128)(2,1)}, bf16[192,2240]{1,0:T(8,128)(2,1)}, u32[]{:S(2)}, u32[]{:S(2)}) collective-permute-start(bf16[192,2240]{1,0:T(8,128)(2,1)} %collective-permute-done.10), channel_id=1, source_target_pairs={{0,4},{4,8},{8,12},{12,16},{16,20},{20,24},{24,28},{28,0},{1,5},{5... | collective-permute-start | bytes 2580488 | tf_op jit(solution)/shard_map/ppermute | solution.py:24
  232.4 396.4 %reduce-scatter.15.cloned.1.call-start = ((), (), s32[]{:S(2)}) async-start(), calls=%async_computation.19 | async-start | bytes 7864320 | tf_op jit(solution)/shard_map/reduce_scatter | solution.py:199
  265.8 35.4 %collective-permute-start.12 = (bf16[192,2240]{1,0:T(8,128)(2,1)}, bf16[192,2240]{1,0:T(8,128)(2,1)S(1)}, u32[]{:S(2)}, u32[]{:S(2)}) collective-permute-start(bf16[192,2240]{1,0:T(8,128)(2,1)} %collective-permute-done.11), channel_id=1, source_target_pairs={{0,4},{4,8},{8,12},{12,16},{16,20},{20,24},{24,28},{28,0},{1,5},{5... | collective-permute-start | bytes 2580488 | tf_op jit(solution)/shard_map/ppermute | solution.py:24
  301.2 37.0 %collective-permute-start.13 = (bf16[192,2240]{1,0:T(8,128)(2,1)S(1)}, bf16[192,2240]{1,0:T(8,128)(2,1)S(1)}, u32[]{:S(2)}, u32[]{:S(2)}) collective-permute-start(bf16[192,2240]{1,0:T(8,128)(2,1)S(1)} %collective-permute-done.12), channel_id=1, source_target_pairs={{0,4},{4,8},{8,12},{12,16},{16,20},{20,24},{24,28},{28,0},{1,5},{5... | collective-permute-start | bytes 2580488 | tf_op jit(solution)/shard_map/ppermute | solution.py:24
  570.2 99.5 %all-gather.23.cloned.1.call-start = ((), (), s32[]{:S(2)}) async-start(), calls=%async_computation.20 | async-start | bytes 3932160 | tf_op jit(solution)/shard_map/all_gather | solution.py:207
  632.2 161.4 %reduce-scatter.27.cloned.1.call-start = ((), (), s32[]{:S(2)}) async-start(), calls=%async_computation.26 | async-start | bytes 7962624 | tf_op jit(solution)/shard_map/reduce_scatter | solution.py:271
  644.6 281.1 %reduce-scatter.25.cloned.1.call-start = ((), (), s32[]{:S(2)}) async-start(), calls=%async_computation.25 | async-start | bytes 7962624 | tf_op jit(solution)/shard_map/reduce_scatter | solution.py:268
  657.2 400.2 %reduce-scatter.29.cloned.1.call-start = ((), (), s32[]{:S(2)}) async-start(), calls=%async_computation.27 | async-start | bytes 7962624 | tf_op jit(solution)/shard_map/reduce_scatter | solution.py:274
  669.7 454.6 %reduce-scatter.23.cloned.1.call-start = ((), (), s32[]{:S(2)}) async-start(), calls=%async_computation.24 | async-start | bytes 1327104 | tf_op jit(solution)/shard_map/reduce_scatter | solution.py:265
  676.2 514.7 %reduce-scatter.19.cloned.1.call-start = ((), (), s32[]{:S(2)}) async-start(), calls=%async_computation.22 | async-start | bytes 1327104 | tf_op jit(solution)/shard_map/reduce_scatter | solution.py:262
  695.8 534.6 %reduce-scatter.17.cloned.1.call-start = ((), (), s32[]{:S(2)}) async-start(), calls=%async_computation.21 | async-start | bytes 3932160 | tf_op jit(solution)/shard_map/reduce_scatter | solution.py:246
  720.6 553.9 %reduce-scatter.13.cloned.1.call-start = ((), (), s32[]{:S(2)}) async-start(), calls=%async_computation.17 | async-start | bytes 3932160 | tf_op jit(solution)/shard_map/reduce_scatter | solution.py:183
  733.2 646.4 %reduce-scatter.21.cloned.1.call-start = ((), (), s32[]{:S(2)}) async-start(), calls=%async_computation.23 | async-start | bytes 3244032 | tf_op jit(solution)/shard_map/reduce_scatter | solution.py:255
  (45 other events, 1832.7 us)
Sparse Core Ops, SparseCore 0:
  11.1 31.2 all-gather.8
  44.5 46.0 all-gather.10
  92.8 39.8 all-gather.12
  138.8 57.1 reduce-scatter.10
  197.4 28.5 all-gather.20
  228.3 145.0 all-gather.18
  375.8 108.3 all-gather.16
  486.3 26.7 all-gather.14
  570.3 58.3 reduce-scatter.14
  632.3 28.5 all-gather.22
  664.6 129.0 reduce-scatter.26
  797.6 128.0 reduce-scatter.24
  929.4 128.0 reduce-scatter.28
  1061.1 63.1 reduce-scatter.22
  1127.8 62.9 reduce-scatter.18
  1193.4 36.9 reduce-scatter.16
  1232.8 38.2 reduce-scatter.12
  1277.8 101.7 reduce-scatter.20
